TPU v7x, 128 devices: a whole 4x4x4 slice. The times are simulated.
128 devices in a mesh: req: 32 (over z, x, core), tp: 4 (over y).
Axes of the slice: x: 4, y: 4, z: 4, core: 2. Of those that a mesh axis runs over, the one named last changes fastest.
Arguments:
- tokens: bfloat16 [12288, 5120], P('req'), may hold values from -40 to 40
- w_query: bfloat16 [5120, 2560], P(None, 'tp'), may hold values from -0.125 to 0.125
- query_bias: float32 [2560], P('tp'), may hold values from -24 to 24
- w_keyval: bfloat16 [5120, 1024], P(None, 'tp'), may hold values from -0.21875 to 0.21875
- keyval_bias: float32 [1024], P('tp'), may hold values from -2.5 to 2.5
- w_out: bfloat16 [2560, 5120], P('tp'), may hold values from -0.25 to 0.25
- attn_gain: float32 [5120], replicated, may hold values from 0.25 to 1.75
- final_norm_gain: float32 [5120], replicated, may hold values from 0.25 to 1.75
- head_weight: bfloat16 [5120, 76032], P(None, ('req', 'tp')), may hold values from -0.25 to 0.25
- kv_pool: bfloat16 [851968, 4, 256], P('req', 'tp'), may hold values from -17 to 17
- cache_len: int32 [512], replicated, may hold values from 256 to 3072, as said below
Outputs:
- states: bfloat16 [12288, 5120], P('req', 'tp')
- new_kv: bfloat16 [12288, 4, 256], P('req', 'tp')
- row_norms: float32 [512], P('req')
- logit_max: float32 [512], replicated
- logits: float32 [512, 76032], P(None, ('req', 'tp'))
Inputs may be any that keep to these rules, and one draw needn't show every extreme that they name: `cache_len`: every cache holds 256 or 3072 rows. Exactly 64 requests hold 3072; requests i * 16 to i * 16 + 15 hold at most 8 of them for every i, and exactly 8 for some i, so their caches fill at most 26624 rows, and exactly 26624 for some i.
All inputs are finite; a program needn't handle non-finite values.
Results may differ from a plain program's by a relative error of at most 0.014.
Values may be sent and summed in bfloat16 or wider, within the bound.
A program may use at most 192 MiB of HBM per device.

v0:
```python
import math
import jax
import jax.numpy as jnp
from jax import lax
from jax.sharding import PartitionSpec as P

HD = 128
GROUP = 5
NEW = 24
LONG = 3072
THETA = 1000000.0
EPS = 1e-06
NEG = -1e30


def rope_rotate(vectors, positions):
    head_width = vectors.shape[-1]
    halfway = head_width // 2
    frequency = THETA ** (-(jnp.arange(halfway, dtype=jnp.float32) * (2.0 / head_width)))
    angles = positions[..., None] * frequency
    cosine = jnp.cos(angles)
    sine_part = jnp.sin(angles)
    front_part = vectors[..., :halfway]
    back_part = vectors[..., halfway:]
    return jnp.concatenate(
        [front_part * cosine - back_part * sine_part, back_part * cosine + front_part * sine_part],
        axis=-1,
    )


def online_update(state_in, scores, value_matrix):
    running_max, totals, weighted = state_in
    new_max = jnp.maximum(running_max, jnp.max(scores, axis=-1))
    rescale = jnp.exp(running_max - new_max)
    weight_matrix = jnp.exp(scores - new_max[..., None])
    totals = totals * rescale + jnp.sum(weight_matrix, axis=-1)
    weighted = weighted * rescale[..., None] + jnp.einsum(
        "amz,zav->amv",
        weight_matrix.astype(jnp.bfloat16),
        value_matrix,
        preferred_element_type=jnp.float32,
    )
    return (new_max, totals, weighted)


def attend_windows(query_rows, pool_part, leading_row, req_starts, req_lens, start_state):
    head_width = query_rows.shape[-1]
    kv_local = query_rows.shape[0]
    query_count = query_rows.shape[1]
    req_count = req_starts.shape[0]
    row_span = query_count // req_count
    part_rows = pool_part.shape[0]
    window_rows = min(LONG, part_rows)
    batch_size = math.gcd(req_count, 4)
    batch_count = req_count // batch_size

    def per_request(query_block, begin, length, state_max, state_totals, state_weighted):
        first = jnp.clip(begin - leading_row, 0, part_rows - window_rows)
        window = lax.dynamic_slice_in_dim(pool_part, first, window_rows, 0)
        row_index = leading_row + first + jnp.arange(window_rows, dtype=jnp.int32)
        inside = (row_index >= begin) & (row_index < begin + length)
        scores = jnp.einsum(
            "mjl,wml->mjw",
            query_block,
            window[..., :head_width],
            preferred_element_type=jnp.float32,
        )
        scores = jnp.where(inside[None, None, :], scores, -jnp.inf)
        return online_update(
            (state_max, state_totals, state_weighted), scores, window[..., head_width:]
        )

    def split_requests(array_in):
        moved = jnp.moveaxis(
            array_in.reshape((kv_local, req_count, row_span) + array_in.shape[2:]), 1, 0
        )
        return moved.reshape((batch_count, batch_size) + moved.shape[1:])

    def join_requests(array_in):
        merged = array_in.reshape((req_count,) + array_in.shape[2:])
        return jnp.moveaxis(merged, 0, 1).reshape((kv_local, query_count) + merged.shape[3:])

    def one_batch(inputs):
        return jax.vmap(per_request)(*inputs)

    batched = (
        split_requests(query_rows),
        req_starts.reshape(batch_count, batch_size),
        req_lens.reshape(batch_count, batch_size),
        split_requests(start_state[0]),
        split_requests(start_state[1]),
        split_requests(start_state[2]),
    )
    result = lax.map(one_batch, batched)
    return tuple((join_requests(part_state) for part_state in result))


def local(
    tokens,
    w_query,
    query_bias,
    w_keyval,
    keyval_bias,
    w_out,
    attn_gain,
    final_norm_gain,
    head_weight,
    kv_pool,
    cache_len,
):
    groups = lax.axis_size("req")
    my_group = lax.axis_index("req")
    tp_count = lax.axis_size("tp")
    tp_index = lax.axis_index("tp")
    tok_rows = tokens.shape[0]
    model_width = tokens.shape[1]
    per_group = tok_rows // NEW
    kv_local = kv_pool.shape[1]
    lens_grid = cache_len.reshape(groups, per_group)
    my_lens = lax.dynamic_slice_in_dim(lens_grid, my_group, 1, 0)[0]
    my_starts = jnp.cumsum(my_lens) - my_lens
    source = tokens.astype(jnp.float32)
    mean_square = jnp.mean(source * source, axis=1, keepdims=True)
    normed = (source / jnp.sqrt(mean_square + EPS) * attn_gain[None, :]).astype(jnp.bfloat16)
    query_raw = jnp.dot(normed, w_query, preferred_element_type=jnp.float32) + query_bias[None, :]
    keyval_raw = (
        jnp.dot(normed, w_keyval, preferred_element_type=jnp.float32) + keyval_bias[None, :]
    )
    positions = (my_lens[:, None] + jnp.arange(NEW, dtype=jnp.int32)[None, :]).astype(jnp.float32)
    query_heads = query_raw.reshape(per_group, NEW, kv_local, GROUP, HD)
    queries = (
        rope_rotate(query_heads, positions[:, :, None, None]) * (1.0 / math.sqrt(HD))
    ).astype(jnp.bfloat16)
    keyval_heads = keyval_raw.reshape(per_group, NEW, kv_local, 2, HD)
    key_new = rope_rotate(keyval_heads[:, :, :, 0, :], positions[:, :, None]).astype(jnp.bfloat16)
    value_new = keyval_heads[:, :, :, 1, :].astype(jnp.bfloat16)
    new_kv = jnp.concatenate([key_new, value_new], axis=-1).reshape(tok_rows, kv_local, 2 * HD)
    row_span = NEW * GROUP
    query_count = per_group * row_span
    query_rows = jnp.transpose(queries, (2, 0, 1, 3, 4)).reshape(kv_local, query_count, HD)
    start_state = (
        jnp.full((kv_local, query_count), NEG, jnp.float32),
        jnp.zeros((kv_local, query_count), jnp.float32),
        jnp.zeros((kv_local, query_count, HD), jnp.float32),
    )
    carry_state = attend_windows(query_rows, kv_pool, 0, my_starts, my_lens, start_state)
    key_rows = key_new.reshape(tok_rows, kv_local, HD)
    value_rows = value_new.reshape(tok_rows, kv_local, HD)
    new_scores = jnp.einsum(
        "kqd,mkd->kqm", query_rows, key_rows, preferred_element_type=jnp.float32
    )
    query_token = jnp.arange(query_count, dtype=jnp.int32) // GROUP
    key_token = jnp.arange(tok_rows, dtype=jnp.int32)
    allowed = (query_token[:, None] // NEW == key_token[None, :] // NEW) & (
        key_token[None, :] <= query_token[:, None]
    )
    new_scores = jnp.where(allowed[None], new_scores, -jnp.inf)
    carry_state = online_update(carry_state, new_scores, value_rows)
    attention = (carry_state[2] / carry_state[1][..., None]).astype(jnp.bfloat16)
    attention = jnp.transpose(
        attention.reshape(kv_local, per_group, NEW, GROUP, HD), (1, 2, 0, 3, 4)
    ).reshape(tok_rows, kv_local * GROUP * HD)
    partial_value = jnp.dot(attention, w_out, preferred_element_type=jnp.float32)
    width_local = model_width // tp_count
    summed = lax.psum(partial_value.astype(jnp.bfloat16), "tp").astype(jnp.float32)
    states_full = (source + summed).astype(jnp.bfloat16)
    states = lax.dynamic_slice_in_dim(states_full, tp_index * width_local, width_local, 1)
    last_rows = states_full.reshape(per_group, NEW, model_width)[:, NEW - 1, :].astype(jnp.float32)
    row_norms = jnp.sqrt(jnp.mean(last_rows * last_rows, axis=1) + EPS)
    final_rows = (last_rows / row_norms[:, None] * final_norm_gain[None, :]).astype(jnp.bfloat16)
    logits = jnp.dot(
        lax.all_gather(final_rows, "req", axis=0, tiled=True),
        head_weight,
        preferred_element_type=jnp.float32,
    )
    logit_max = lax.pmax(jnp.max(logits, axis=1), ("req", "tp"))
    return (states, new_kv, row_norms, logit_max, logits)


def solution(mesh):
    return jax.shard_map(
        local,
        mesh=mesh,
        in_specs=(
            P("req", None),
            P(None, "tp"),
            P("tp"),
            P(None, "tp"),
            P("tp"),
            P("tp", None),
            P(),
            P(),
            P(None, ("req", "tp")),
            P("req", "tp", None),
            P(),
        ),
        out_specs=(P("req", "tp"), P("req", "tp", None), P("req"), P(), P(None, ("req", "tp"))),
        check_vma=False,
    )
```

profile of v0, /device:TPU:1, one launch (start us, length us, event | category | flops | bytes accessed | tf_op | source)
XLA Modules:
  0.0 365.2 jit_solution(11805179985593253152)
XLA Ops:
  7.3 3.1 fusion.27
  10.7 3.6 fusion.29
  16.1 4.2 %convolution_add_fusion.1 = f32[384,640]{1,0:T(8,128)} fusion(bf16[384,5120]{1,0:T(8,128)(2,1)S(1)} %fusion.29, bf16[5120,640]{1,0:T(8,128)(2,1)S(1)} %copy-done.12, f32[640]{0:T(1024)S(1)} %copy-done.13), kind=kOutput, calls=%fused_computation.58 | convolution fusion | flops 2516828160 | bytes 11471360 | tf_op jit(solution)/shard_map/dot_general | solution.py:125
  23.5 4.2 %multiply_subtract_fusion = (f32[16,24,1,5,64]{4,3,1,0,2:T(8,128)}, f32[16,24,1,5,64]{4,3,1,0,2:T(8,128)}) fusion(f32[16,24,1,5,128]{4,3,1,0,2:T(8,128)} %reshape.555, f32[16,24,64]{2,1,0:T(8,128)S(1)} %get-tuple-element.120, f32[16,24,64]{2,1,0:T(8,128)S(1)} %get-tuple-element.119), kind=kLoop, calls=%fused_computation.56 | loop fusion | flops 737280 | bytes 2162688 | tf_op jit(solution)/shard_map/sub | solution.py:26
  38.9 3.3 convolution_add_fusion.2
  45.7 81.0 %while.17 = (s32[]{:T(128)}, f32[4,4,1,120]{3,1,2,0:T(4,128)S(1)}, f32[4,4,1,120]{3,1,2,0:T(4,128)S(1)}, f32[4,4,1,120,128]{4,3,1,2,0:T(8,128)}, s32[4,4]{1,0:T(...) while((s32[]{:T(128)}, f32[4,4,1,120]{3,1,2,0:T(4,128)S(1)}, ...), condition=%wide.region_5.6_spmd, body=%wide.region_2.5_spmd.sunk | while | flops 766884224 | bytes 52985684 | solution.py:94
  46.1 12.2 %while.18 = (s32[]{:T(128)}, bf16[26624,1,256]{2,0,1:T(8,128)(2,1)}, s32[4,3]{1,0:T(4,128)S(1)}, bf16[4,3072,1,256]{3,1,2,0:T(8,128)(2,1)}, s32[]{:T(128)}) while((s32[]{:T(128)}, bf16[26624,1,256]{2,0,1:T(8,128)(2,1)}, s32[4,3]{1,0:T(4,128)S(1)}, bf16[4,3072,1,256]{3,1,2,0:T(8,128)(2,1)}, s32[]{:T(128)}) %tuple.62), condition=%wide.while_cond, body=%wide.while_body.sunk | while | flops 2 | bytes 3145833 | solution.py:59
  46.1 3.2 bitcast_dynamic-update-slice_fusion.3
  49.3 3.0 bitcast_dynamic-update-slice_fusion.3
  55.3 3.0 bitcast_dynamic-update-slice_fusion.3
  58.3 4.2 %select_reduce_fusion.2 = (f32[4,120]{1,0:T(4,128)S(1)}, f32[4,120,3072]{2,1,0:T(8,128)S(1)}) fusion(pred[4,3072]{1,0:T(4,128)(4,1)S(1)} %fusion.90, bf16[4,3072,1,256]{3,1,0,2:T(8,128)(2,1)} %bitcast.118, bf16[1,4,1,120,128]{4,1,0,3,2:T(4,128)(2,1)S(1)} %constant_dynamic-slice_fusion.8), kind=kOutput, calls=%fused_computation.3.clone.1 | convolution fusion | flops 380436000 | bytes 9181056 | tf_op jit(solution)/shard_map/while/body/eval_jaxpr/vmap(mjl,wml->mjw)/dot_general | solution.py:62
  66.4 12.1 %while.18 = (s32[]{:T(128)}, bf16[26624,1,256]{2,0,1:T(8,128)(2,1)}, s32[4,3]{1,0:T(4,128)S(1)}, bf16[4,3072,1,256]{3,1,2,0:T(8,128)(2,1)}, s32[]{:T(128)}) while((s32[]{:T(128)}, bf16[26624,1,256]{2,0,1:T(8,128)(2,1)}, s32[4,3]{1,0:T(4,128)S(1)}, bf16[4,3072,1,256]{3,1,2,0:T(8,128)(2,1)}, s32[]{:T(128)}) %tuple.62), condition=%wide.while_cond, body=%wide.while_body.sunk | while | flops 2 | bytes 3145833 | solution.py:59
  66.4 3.0 bitcast_dynamic-update-slice_fusion.3
  75.4 3.0 bitcast_dynamic-update-slice_fusion.3
  78.4 4.2 %select_reduce_fusion.2 = (f32[4,120]{1,0:T(4,128)S(1)}, f32[4,120,3072]{2,1,0:T(8,128)S(1)}) fusion(pred[4,3072]{1,0:T(4,128)(4,1)S(1)} %fusion.90, bf16[4,3072,1,256]{3,1,0,2:T(8,128)(2,1)} %bitcast.118, bf16[1,4,1,120,128]{4,1,0,3,2:T(4,128)(2,1)S(1)} %constant_dynamic-slice_fusion.8), kind=kOutput, calls=%fused_computation.3.clone.1 | convolution fusion | flops 380436000 | bytes 9181056 | tf_op jit(solution)/shard_map/while/body/eval_jaxpr/vmap(mjl,wml->mjw)/dot_general | solution.py:62
  86.5 12.1 %while.18 = (s32[]{:T(128)}, bf16[26624,1,256]{2,0,1:T(8,128)(2,1)}, s32[4,3]{1,0:T(4,128)S(1)}, bf16[4,3072,1,256]{3,1,2,0:T(8,128)(2,1)}, s32[]{:T(128)}) while((s32[]{:T(128)}, bf16[26624,1,256]{2,0,1:T(8,128)(2,1)}, s32[4,3]{1,0:T(4,128)S(1)}, bf16[4,3072,1,256]{3,1,2,0:T(8,128)(2,1)}, s32[]{:T(128)}) %tuple.62), condition=%wide.while_cond, body=%wide.while_body.sunk | while | flops 2 | bytes 3145833 | solution.py:59
  86.5 3.0 bitcast_dynamic-update-slice_fusion.3
  89.6 3.0 bitcast_dynamic-update-slice_fusion.3
  95.6 3.0 bitcast_dynamic-update-slice_fusion.3
  98.6 4.2 %select_reduce_fusion.2 = (f32[4,120]{1,0:T(4,128)S(1)}, f32[4,120,3072]{2,1,0:T(8,128)S(1)}) fusion(pred[4,3072]{1,0:T(4,128)(4,1)S(1)} %fusion.90, bf16[4,3072,1,256]{3,1,0,2:T(8,128)(2,1)} %bitcast.118, bf16[1,4,1,120,128]{4,1,0,3,2:T(4,128)(2,1)S(1)} %constant_dynamic-slice_fusion.8), kind=kOutput, calls=%fused_computation.3.clone.1 | convolution fusion | flops 380436000 | bytes 9181056 | tf_op jit(solution)/shard_map/while/body/eval_jaxpr/vmap(mjl,wml->mjw)/dot_general | solution.py:62
  106.7 12.1 %while.18 = (s32[]{:T(128)}, bf16[26624,1,256]{2,0,1:T(8,128)(2,1)}, s32[4,3]{1,0:T(4,128)S(1)}, bf16[4,3072,1,256]{3,1,2,0:T(8,128)(2,1)}, s32[]{:T(128)}) while((s32[]{:T(128)}, bf16[26624,1,256]{2,0,1:T(8,128)(2,1)}, s32[4,3]{1,0:T(4,128)S(1)}, bf16[4,3072,1,256]{3,1,2,0:T(8,128)(2,1)}, s32[]{:T(128)}) %tuple.62), condition=%wide.while_cond, body=%wide.while_body.sunk | while | flops 2 | bytes 3145833 | solution.py:59
  106.7 3.0 bitcast_dynamic-update-slice_fusion.3
  109.7 3.0 bitcast_dynamic-update-slice_fusion.3
  112.7 3.0 bitcast_dynamic-update-slice_fusion.3
  115.7 3.0 bitcast_dynamic-update-slice_fusion.3
  118.7 4.2 %select_reduce_fusion.2 = (f32[4,120]{1,0:T(4,128)S(1)}, f32[4,120,3072]{2,1,0:T(8,128)S(1)}) fusion(pred[4,3072]{1,0:T(4,128)(4,1)S(1)} %fusion.90, bf16[4,3072,1,256]{3,1,0,2:T(8,128)(2,1)} %bitcast.118, bf16[1,4,1,120,128]{4,1,0,3,2:T(4,128)(2,1)S(1)} %constant_dynamic-slice_fusion.8), kind=kOutput, calls=%fused_computation.3.clone.1 | convolution fusion | flops 380436000 | bytes 9181056 | tf_op jit(solution)/shard_map/while/body/eval_jaxpr/vmap(mjl,wml->mjw)/dot_general | solution.py:62
  129.9 7.6 %convolution_convert_fusion = bf16[384,5120]{1,0:T(8,128)(2,1)} fusion(bf16[384,640]{1,0:T(8,128)(2,1)S(1)} %reshape_transpose_reshape.16, bf16[640,5120]{1,0:T(8,128)(2,1)} %param.18), kind=kOutput, calls=%fused_computation.45 | convolution fusion | flops 2518548480 | bytes 10977280 | tf_op jit(solution)/shard_map/dot_general | solution.py:163
  137.5 91.8 %all-reduce.3.cloned.1.call-done = bf16[384,5120]{1,0:T(8,128)(2,1)} async-done(((bf16[384,5120]{1,0:T(8,128)(2,1)}), bf16[384,5120]{1,0:T(8,128)(2,1)}) %all-reduce.3.cloned.1.call-update) | async-done | bytes 3932176 | tf_op jit(solution)/shard_map/psum | solution.py:165
  229.4 4.8 %fusion.30 = bf16[384,5120]{1,0:T(8,128)(2,1)S(1)} fusion(bf16[384,5120]{1,0:T(8,128)(2,1)} %param.13, bf16[384,5120]{1,0:T(8,128)(2,1)} %all-reduce.3.cloned.1.call-done), kind=kLoop, calls=%fused_computation.44 | loop fusion | flops 7864320 | bytes 11796480 | tf_op jit(solution)/shard_map/convert_element_type | solution.py:166
  240.4 44.9 %all-gather.2.cloned.1.call-done = bf16[512,5120]{1,0:T(8,128)(2,1)} async-done(((bf16[16,5120]{1,0:T(8,128)(2,1)}), bf16[512,5120]{1,0:T(8,128)(2,1)}) %all-gather.2.cloned.1.call-update) | async-done | bytes 5242896 | tf_op jit(solution)/shard_map/all_gather | solution.py:172
  285.3 8.8 %fusion.72 = (f32[512]{0:T(512)S(1)}, f32[512,594]{0,1:T(8,128)}) fusion(bf16[512,5120]{1,0:T(8,128)(2,1)} %all-gather.2.cloned.1.call-done, bf16[5120,594]{0,1:T(8,128)(2,1)} %param.21), kind=kOutput, calls=%fused_computation.122 | convolution fusion | flops 3114574336 | bytes 12544000 | tf_op jit(solution)/shard_map/dot_general | solution.py:171
  294.2 64.1 %pmax.7 = f32[512]{0:T(512)} all-reduce(f32[512]{0:T(512)S(1)} %get-tuple-element.123), channel_id=1, replica_groups=mesh['req'=32,'tp'=4] {'req','tp'}, use_global_device_ids=true, to_apply=%region_11.12 | all-reduce | flops 512 | bytes 4096 | tf_op jit(solution)/shard_map/pmax | solution.py:176
  (150 shorter events, 56.6 us)
Async XLA Ops:
  7.2 31.7 %copy-start = (bf16[5120,256]{1,0:T(8,128)(2,1)S(1)}, bf16[5120,256]{1,0:T(8,128)(2,1)}, u32[]{:S(2)}) copy-start(bf16[5120,256]{1,0:T(8,128)(2,1)} %param.16) | copy-start | bytes 7864324
  7.2 3.3 copy-start.10
  7.2 3.5 copy-start.8
  7.2 222.2 %all-reduce.3.cloned.1.call-start = ((), (), s32[]{:S(2)}) async-start(), calls=%async_computation | async-start | bytes 7864320 | tf_op jit(solution)/shard_map/psum | solution.py:165
  10.6 5.5 %copy-start.12 = (bf16[5120,640]{1,0:T(8,128)(2,1)S(1)}, bf16[5120,640]{1,0:T(8,128)(2,1)}, u32[]{:S(2)}) copy-start(bf16[5120,640]{1,0:T(8,128)(2,1)} %param.14) | copy-start | bytes 19660804
  10.7 5.5 %copy-start.13 = (f32[640]{0:T(1024)S(1)}, f32[640]{0:T(1024)}, u32[]{:S(2)}) copy-start(f32[640]{0:T(1024)} %param.15) | copy-start | bytes 7684
  14.2 1.9 copy-start.4
  30.1 8.8 %copy-start.14 = (f32[256]{0:T(256)S(1)}, f32[256]{0:T(256)}, u32[]{:S(2)}) copy-start(f32[256]{0:T(256)} %param.17) | copy-start | bytes 3076
  45.7 81.2 %copy-start.5 = (f32[1920,64]{1,0:T(8,128)S(1)}, f32[1920,64]{1,0:T(8,128)}, u32[]{:S(2)}) copy-start(f32[1920,64]{1,0:T(8,128)} %concatenate.59) | copy-start | bytes 1474564
  45.7 81.2 %copy-start.6 = (f32[1920,64]{1,0:T(8,128)S(1)}, f32[1920,64]{1,0:T(8,128)}, u32[]{:S(2)}) copy-start(f32[1920,64]{1,0:T(8,128)} %concatenate.60) | copy-start | bytes 1474564
  58.3 4.3 %copy-start.2 = (bf16[4,3072,1,256]{3,1,2,0:T(8,128)(2,1)S(1)}, bf16[4,3072,1,256]{3,1,2,0:T(8,128)(2,1)}, u32[]{:S(2)}) copy-start(bf16[4,3072,1,256]{3,1,2,0:T(8,128)(2,1)} %get-tuple-element.216) | copy-start | bytes 18874372 | tf_op jit(solution)/shard_map/while
  78.4 4.2 %copy-start.2 = (bf16[4,3072,1,256]{3,1,2,0:T(8,128)(2,1)S(1)}, bf16[4,3072,1,256]{3,1,2,0:T(8,128)(2,1)}, u32[]{:S(2)}) copy-start(bf16[4,3072,1,256]{3,1,2,0:T(8,128)(2,1)} %get-tuple-element.216) | copy-start | bytes 18874372 | tf_op jit(solution)/shard_map/while
  98.6 4.2 %copy-start.2 = (bf16[4,3072,1,256]{3,1,2,0:T(8,128)(2,1)S(1)}, bf16[4,3072,1,256]{3,1,2,0:T(8,128)(2,1)}, u32[]{:S(2)}) copy-start(bf16[4,3072,1,256]{3,1,2,0:T(8,128)(2,1)} %get-tuple-element.216) | copy-start | bytes 18874372 | tf_op jit(solution)/shard_map/while
  118.7 4.2 %copy-start.2 = (bf16[4,3072,1,256]{3,1,2,0:T(8,128)(2,1)S(1)}, bf16[4,3072,1,256]{3,1,2,0:T(8,128)(2,1)}, u32[]{:S(2)}) copy-start(bf16[4,3072,1,256]{3,1,2,0:T(8,128)(2,1)} %get-tuple-element.216) | copy-start | bytes 18874372 | tf_op jit(solution)/shard_map/while
  126.9 1.5 copy-start.7
  137.5 99.1 %copy-start.9 = (f32[5120]{0:T(1024)S(1)}, f32[5120]{0:T(1024)}, u32[]{:S(2)}) copy-start(f32[5120]{0:T(1024)} %param.20) | copy-start | bytes 61444
  137.5 147.8 %all-gather.2.cloned.1.call-start = ((), (), s32[]{:S(2)}) async-start(), calls=%async_computation.1 | async-start | bytes 5406720 | tf_op jit(solution)/shard_map/all_gather | solution.py:172
  234.2 1.9 copy-start.3
  236.6 57.6 %copy-start.11 = (f32[16]{0:T(128)}, f32[16]{0:T(128)S(1)}, u32[]{:S(2)}) copy-start(f32[16]{0:T(128)S(1)} %add_sqrt_fusion.1) | copy-start | bytes 196
  285.3 73.0 %copy-start.1 = (bf16[5120,256]{1,0:T(8,128)(2,1)S(1)}, bf16[5120,256]{1,0:T(8,128)(2,1)}, u32[]{:S(2)}) copy-start(bf16[5120,256]{1,0:T(8,128)(2,1)} %param.16) | copy-start | bytes 7864324
Sparse Core Ops, SparseCore 0:
  137.6 91.7 all-reduce.2
  237.5 47.7 all-gather.1
where the time goes:
time: 366 us; the launch traced here: 365 us
  waiting for transfers between devices  137 us (37%)
  local copies, waits for them, and re-layouts  69.7 us (19%)
  blocking collectives  64.1 us (18%)
  matrix products  51.4 us (14%)
  other arithmetic  28.1 us (8%)
  between operations  14.4 us (4%)
    psum x1, waiting for transfers between devices, local(): lax.psum(partial_value.astype(jnp.bfloat16), 'tp').astype(jnp.float32)  91.8 us
    pmax x1, blocking collectives, local(): logit_max = lax.pmax(jnp.max(logits, axis=1), ('req', 'tp'))  64.1 us
    gather x32, local copies, waits for them, and re-layouts  48.3 us
    all_gather x1, waiting for transfers between devices, local(): lax.all_gather(final_rows, 'req', axis=0, tiled=True)  44.9 us
    dot_general x4, matrix products, per_request(): jnp.einsum('mjl,wml->mjw', query_block, window[..., :head_width], preferr...  16.9 us
    dot_general x5, matrix products, online_update(): jnp.einsum('amz,zav->amv', weight_matrix.astype(jnp.bfloat16), value_matr...  9.56 us
    dot_general x1, matrix products, local(): jnp.dot(lax.all_gather(final_rows, 'req', axis=0, tiled=True), head_weigh...  8.84 us
    dot_general x1, matrix products, local(): jnp.dot(attention, w_out, preferred_element_type=jnp.float32)  7.58 us
  transfers between devices with their start and end apart: 2, of which 2 were waited for; matrix products, arithmetic and copies ran while one was open for 1% of the time, Pallas kernels for 0%

commit v1 on v0

--- a/solution.py
+++ b/solution.py
@@ -169,7 +169,15 @@
     row_norms = jnp.sqrt(jnp.mean(last_rows * last_rows, axis=1) + EPS)
     final_rows = (last_rows / row_norms[:, None] * final_norm_gain[None, :]).astype(jnp.bfloat16)
     logits = jnp.dot(
-        lax.all_gather(final_rows, "req", axis=0, tiled=True),
+        jnp.concatenate(
+            lax.all_to_all(
+                jnp.stack([final_rows for _ in range(lax.axis_size("req"))]),
+                split_axis=0,
+                concat_axis=0,
+                axis_name="req",
+            ),
+            0,
+        ),
         head_weight,
         preferred_element_type=jnp.float32,
     )

time: 366 us -> 392 us (1.071)
  waiting for transfers between devices: 137 us -> 150 us
  starting transfers between devices: 0.08 us -> 7.76 us
    all_to_all x0 -> x1, waiting for transfers between devices: none -> 58.5 us  [local(): lax.all_to_all(jnp.stack([final_rows for _ in range(lax.axis_size('req'))...]
    all_gather x1 -> x0, waiting for transfers between devices: 44.9 us -> none  [local(): lax.all_gather(final_rows, 'req', axis=0, tiled=True)]
    all_to_all x0 -> x1, starting transfers between devices: none -> 7.72 us  [local(): lax.all_to_all(jnp.stack([final_rows for _ in range(lax.axis_size('req'))...]
where the time goes in v1:
time: 392 us; the launch traced here: 391 us
  waiting for transfers between devices  150 us (38%)
  local copies, waits for them, and re-layouts  72.6 us (19%)
  blocking collectives  66.5 us (17%)
  matrix products  51.4 us (13%)
  other arithmetic  27.4 us (7%)
  between operations  14.4 us (4%)
  starting transfers between devices  7.76 us (2%)
    psum x1, waiting for transfers between devices, local(): lax.psum(partial_value.astype(jnp.bfloat16), 'tp').astype(jnp.float32)  91.9 us
    pmax x1, blocking collectives, local(): logit_max = lax.pmax(jnp.max(logits, axis=1), ('req', 'tp'))  66.5 us
    all_to_all x1, waiting for transfers between devices, local(): lax.all_to_all(jnp.stack([final_rows for _ in range(lax.axis_size('req'))...  58.5 us
    gather x32, local copies, waits for them, and re-layouts  48.2 us
    dot_general x4, matrix products, per_request(): jnp.einsum('mjl,wml->mjw', query_block, window[..., :head_width], preferr...  16.9 us
    dot_general x5, matrix products, online_update(): jnp.einsum('amz,zav->amv', weight_matrix.astype(jnp.bfloat16), value_matr...  9.57 us
    dot_general x1, matrix products, local(): jnp.dot(jnp.concatenate(lax.all_to_all(jnp.stack([final_rows for _ in ran...  8.84 us
  transfers between devices with their start and end apart: 2, of which 2 were waited for; matrix products, arithmetic and copies ran while one was open for 1% of the time, Pallas kernels for 0%

profile of v1, /device:TPU:1, one launch (start us, length us, event | category | flops | bytes accessed | tf_op | source)
XLA Modules:
  0.0 391.1 jit_solution(7699761293110443719)
XLA Ops:
  7.3 3.1 fusion.27
  10.7 3.6 fusion.29
  16.1 4.2 %convolution_add_fusion.1 = f32[384,640]{1,0:T(8,128)} fusion(bf16[384,5120]{1,0:T(8,128)(2,1)S(1)} %fusion.29, bf16[5120,640]{1,0:T(8,128)(2,1)S(1)} %copy-done.12, f32[640]{0:T(1024)S(1)} %copy-done.13), kind=kOutput, calls=%fused_computation.58 | convolution fusion | flops 2516828160 | bytes 11471360 | tf_op jit(solution)/shard_map/dot_general | solution.py:125
  23.5 4.1 %multiply_subtract_fusion = (f32[16,24,1,5,64]{4,3,1,0,2:T(8,128)}, f32[16,24,1,5,64]{4,3,1,0,2:T(8,128)}) fusion(f32[16,24,1,5,128]{4,3,1,0,2:T(8,128)} %reshape.576, f32[16,24,64]{2,1,0:T(8,128)S(1)} %get-tuple-element.120, f32[16,24,64]{2,1,0:T(8,128)S(1)} %get-tuple-element.119), kind=kLoop, calls=%fused_computation.56 | loop fusion | flops 737280 | bytes 2162688 | tf_op jit(solution)/shard_map/sub | solution.py:26
  38.9 3.3 convolution_add_fusion.2
  45.7 80.9 %while.17 = (s32[]{:T(128)}, f32[4,4,1,120]{3,1,2,0:T(4,128)S(1)}, f32[4,4,1,120]{3,1,2,0:T(4,128)S(1)}, f32[4,4,1,120,128]{4,3,1,2,0:T(8,128)}, s32[4,4]{1,0:T(...) while((s32[]{:T(128)}, f32[4,4,1,120]{3,1,2,0:T(4,128)S(1)}, ...), condition=%wide.region_5.6_spmd, body=%wide.region_2.5_spmd.sunk | while | flops 766884224 | bytes 52985684 | solution.py:94
  46.0 12.2 %while.18 = (s32[]{:T(128)}, bf16[26624,1,256]{2,0,1:T(8,128)(2,1)}, s32[4,3]{1,0:T(4,128)S(1)}, bf16[4,3072,1,256]{3,1,2,0:T(8,128)(2,1)}, s32[]{:T(128)}) while((s32[]{:T(128)}, bf16[26624,1,256]{2,0,1:T(8,128)(2,1)}, s32[4,3]{1,0:T(4,128)S(1)}, bf16[4,3072,1,256]{3,1,2,0:T(8,128)(2,1)}, s32[]{:T(128)}) %tuple.62), condition=%wide.while_cond, body=%wide.while_body.sunk | while | flops 2 | bytes 3145833 | solution.py:59
  46.1 3.2 bitcast_dynamic-update-slice_fusion.3
  49.2 3.0 bitcast_dynamic-update-slice_fusion.3
  55.2 3.0 bitcast_dynamic-update-slice_fusion.3
  58.3 4.2 %select_reduce_fusion.2 = (f32[4,120]{1,0:T(4,128)S(1)}, f32[4,120,3072]{2,1,0:T(8,128)S(1)}) fusion(pred[4,3072]{1,0:T(4,128)(4,1)S(1)} %fusion.90, bf16[4,3072,1,256]{3,1,0,2:T(8,128)(2,1)} %bitcast.119, bf16[1,4,1,120,128]{4,1,0,3,2:T(4,128)(2,1)S(1)} %constant_dynamic-slice_fusion.8), kind=kOutput, calls=%fused_computation.3.clone.1 | convolution fusion | flops 380436000 | bytes 9181056 | tf_op jit(solution)/shard_map/while/body/eval_jaxpr/vmap(mjl,wml->mjw)/dot_general | solution.py:62
  66.3 12.0 %while.18 = (s32[]{:T(128)}, bf16[26624,1,256]{2,0,1:T(8,128)(2,1)}, s32[4,3]{1,0:T(4,128)S(1)}, bf16[4,3072,1,256]{3,1,2,0:T(8,128)(2,1)}, s32[]{:T(128)}) while((s32[]{:T(128)}, bf16[26624,1,256]{2,0,1:T(8,128)(2,1)}, s32[4,3]{1,0:T(4,128)S(1)}, bf16[4,3072,1,256]{3,1,2,0:T(8,128)(2,1)}, s32[]{:T(128)}) %tuple.62), condition=%wide.while_cond, body=%wide.while_body.sunk | while | flops 2 | bytes 3145833 | solution.py:59
  66.4 3.0 bitcast_dynamic-update-slice_fusion.3
  69.4 3.0 bitcast_dynamic-update-slice_fusion.3
  75.4 3.0 bitcast_dynamic-update-slice_fusion.3
  78.4 4.2 %select_reduce_fusion.2 = (f32[4,120]{1,0:T(4,128)S(1)}, f32[4,120,3072]{2,1,0:T(8,128)S(1)}) fusion(pred[4,3072]{1,0:T(4,128)(4,1)S(1)} %fusion.90, bf16[4,3072,1,256]{3,1,0,2:T(8,128)(2,1)} %bitcast.119, bf16[1,4,1,120,128]{4,1,0,3,2:T(4,128)(2,1)S(1)} %constant_dynamic-slice_fusion.8), kind=kOutput, calls=%fused_computation.3.clone.1 | convolution fusion | flops 380436000 | bytes 9181056 | tf_op jit(solution)/shard_map/while/body/eval_jaxpr/vmap(mjl,wml->mjw)/dot_general | solution.py:62
  86.5 12.0 %while.18 = (s32[]{:T(128)}, bf16[26624,1,256]{2,0,1:T(8,128)(2,1)}, s32[4,3]{1,0:T(4,128)S(1)}, bf16[4,3072,1,256]{3,1,2,0:T(8,128)(2,1)}, s32[]{:T(128)}) while((s32[]{:T(128)}, bf16[26624,1,256]{2,0,1:T(8,128)(2,1)}, s32[4,3]{1,0:T(4,128)S(1)}, bf16[4,3072,1,256]{3,1,2,0:T(8,128)(2,1)}, s32[]{:T(128)}) %tuple.62), condition=%wide.while_cond, body=%wide.while_body.sunk | while | flops 2 | bytes 3145833 | solution.py:59
  86.5 3.0 bitcast_dynamic-update-slice_fusion.3
  89.5 3.0 bitcast_dynamic-update-slice_fusion.3
  95.5 3.0 bitcast_dynamic-update-slice_fusion.3
  98.5 4.2 %select_reduce_fusion.2 = (f32[4,120]{1,0:T(4,128)S(1)}, f32[4,120,3072]{2,1,0:T(8,128)S(1)}) fusion(pred[4,3072]{1,0:T(4,128)(4,1)S(1)} %fusion.90, bf16[4,3072,1,256]{3,1,0,2:T(8,128)(2,1)} %bitcast.119, bf16[1,4,1,120,128]{4,1,0,3,2:T(4,128)(2,1)S(1)} %constant_dynamic-slice_fusion.8), kind=kOutput, calls=%fused_computation.3.clone.1 | convolution fusion | flops 380436000 | bytes 9181056 | tf_op jit(solution)/shard_map/while/body/eval_jaxpr/vmap(mjl,wml->mjw)/dot_general | solution.py:62
  106.6 12.0 %while.18 = (s32[]{:T(128)}, bf16[26624,1,256]{2,0,1:T(8,128)(2,1)}, s32[4,3]{1,0:T(4,128)S(1)}, bf16[4,3072,1,256]{3,1,2,0:T(8,128)(2,1)}, s32[]{:T(128)}) while((s32[]{:T(128)}, bf16[26624,1,256]{2,0,1:T(8,128)(2,1)}, s32[4,3]{1,0:T(4,128)S(1)}, bf16[4,3072,1,256]{3,1,2,0:T(8,128)(2,1)}, s32[]{:T(128)}) %tuple.62), condition=%wide.while_cond, body=%wide.while_body.sunk | while | flops 2 | bytes 3145833 | solution.py:59
  106.6 3.0 bitcast_dynamic-update-slice_fusion.3
  115.6 3.0 bitcast_dynamic-update-slice_fusion.3
  118.6 4.2 %select_reduce_fusion.2 = (f32[4,120]{1,0:T(4,128)S(1)}, f32[4,120,3072]{2,1,0:T(8,128)S(1)}) fusion(pred[4,3072]{1,0:T(4,128)(4,1)S(1)} %fusion.90, bf16[4,3072,1,256]{3,1,0,2:T(8,128)(2,1)} %bitcast.119, bf16[1,4,1,120,128]{4,1,0,3,2:T(4,128)(2,1)S(1)} %constant_dynamic-slice_fusion.8), kind=kOutput, calls=%fused_computation.3.clone.1 | convolution fusion | flops 380436000 | bytes 9181056 | tf_op jit(solution)/shard_map/while/body/eval_jaxpr/vmap(mjl,wml->mjw)/dot_general | solution.py:62
  129.8 7.6 %convolution_convert_fusion = bf16[384,5120]{1,0:T(8,128)(2,1)} fusion(bf16[384,640]{1,0:T(8,128)(2,1)S(1)} %reshape_transpose_reshape.16, bf16[640,5120]{1,0:T(8,128)(2,1)} %param.18), kind=kOutput, calls=%fused_computation.45 | convolution fusion | flops 2518548480 | bytes 10977280 | tf_op jit(solution)/shard_map/dot_general | solution.py:163
  137.4 91.9 %all-reduce.3.cloned.1.call-done = bf16[384,5120]{1,0:T(8,128)(2,1)} async-done(((bf16[384,5120]{1,0:T(8,128)(2,1)}), bf16[384,5120]{1,0:T(8,128)(2,1)}) %all-reduce.3.cloned.1.call-update) | async-done | bytes 3932176 | tf_op jit(solution)/shard_map/psum | solution.py:165
  229.3 4.8 %fusion.30 = bf16[384,5120]{1,0:T(8,128)(2,1)S(1)} fusion(bf16[384,5120]{1,0:T(8,128)(2,1)} %param.13, bf16[384,5120]{1,0:T(8,128)(2,1)} %all-reduce.3.cloned.1.call-done), kind=kLoop, calls=%fused_computation.44 | loop fusion | flops 7864320 | bytes 11796480 | tf_op jit(solution)/shard_map/convert_element_type | solution.py:166
  239.6 7.7 %all-to-all-start = ((bf16[32,16,5120]{2,1,0:T(8,128)(2,1)}), bf16[32,16,5120]{2,1,0:T(8,128)(2,1)}, u32[]{:S(2)}, u32[]{:S(2)}) async-start(bf16[32,16,5120]{2,1,0:T(8,128)(2,1)} %stack.2), calls=%async_computation | async-start | bytes 10485760 | tf_op jit(solution)/shard_map/all_to_all | solution.py:173
  250.4 58.5 %all-to-all-done = bf16[32,16,5120]{2,1,0:T(8,128)(2,1)} async-done(((bf16[32,16,5120]{2,1,0:T(8,128)(2,1)}), bf16[32,16,5120]{2,1,0:T(8,128)(2,1)}, u32[]{:S(2)}, u32[]{:S(2)}) %all-to-all-start) | async-done | bytes 5242912 | tf_op jit(solution)/shard_map/all_to_all | solution.py:173
  308.9 8.8 %fusion.72 = (f32[512]{0:T(512)S(1)}, f32[512,594]{0,1:T(8,128)}) fusion(bf16[512,5120]{1,0:T(8,128)(2,1)} %bitcast.24, bf16[5120,594]{0,1:T(8,128)(2,1)} %param.21), kind=kOutput, calls=%fused_computation.122 | convolution fusion | flops 3114574336 | bytes 12544000 | tf_op jit(solution)/shard_map/dot_general | solution.py:171
  317.7 66.5 %pmax.7 = f32[512]{0:T(512)} all-reduce(f32[512]{0:T(512)S(1)} %get-tuple-element.123), channel_id=1, replica_groups=mesh['req'=32,'tp'=4] {'req','tp'}, use_global_device_ids=true, to_apply=%region_11.12 | all-reduce | flops 512 | bytes 4096 | tf_op jit(solution)/shard_map/pmax | solution.py:184
  (150 shorter events, 61.9 us)
Async XLA Ops:
  7.2 31.7 %copy-start = (bf16[5120,256]{1,0:T(8,128)(2,1)S(1)}, bf16[5120,256]{1,0:T(8,128)(2,1)}, u32[]{:S(2)}) copy-start(bf16[5120,256]{1,0:T(8,128)(2,1)} %param.16) | copy-start | bytes 7864324
  7.2 3.3 copy-start.10
  7.2 3.5 copy-start.8
  7.2 222.1 %all-reduce.3.cloned.1.call-start = ((), (), s32[]{:S(2)}) async-start(), calls=%async_computation.1 | async-start | bytes 7864320 | tf_op jit(solution)/shard_map/psum | solution.py:165
  10.6 5.5 %copy-start.12 = (bf16[5120,640]{1,0:T(8,128)(2,1)S(1)}, bf16[5120,640]{1,0:T(8,128)(2,1)}, u32[]{:S(2)}) copy-start(bf16[5120,640]{1,0:T(8,128)(2,1)} %param.14) | copy-start | bytes 19660804
  10.7 5.5 %copy-start.13 = (f32[640]{0:T(1024)S(1)}, f32[640]{0:T(1024)}, u32[]{:S(2)}) copy-start(f32[640]{0:T(1024)} %param.15) | copy-start | bytes 7684
  14.2 1.9 copy-start.4
  30.0 8.8 %copy-start.14 = (f32[256]{0:T(256)S(1)}, f32[256]{0:T(256)}, u32[]{:S(2)}) copy-start(f32[256]{0:T(256)} %param.17) | copy-start | bytes 3076
  45.7 81.1 %copy-start.5 = (f32[1920,64]{1,0:T(8,128)S(1)}, f32[1920,64]{1,0:T(8,128)}, u32[]{:S(2)}) copy-start(f32[1920,64]{1,0:T(8,128)} %concatenate.59) | copy-start | bytes 1474564
  45.7 81.1 %copy-start.6 = (f32[1920,64]{1,0:T(8,128)S(1)}, f32[1920,64]{1,0:T(8,128)}, u32[]{:S(2)}) copy-start(f32[1920,64]{1,0:T(8,128)} %concatenate.60) | copy-start | bytes 1474564
  58.3 4.2 %copy-start.2 = (bf16[4,3072,1,256]{3,1,2,0:T(8,128)(2,1)S(1)}, bf16[4,3072,1,256]{3,1,2,0:T(8,128)(2,1)}, u32[]{:S(2)}) copy-start(bf16[4,3072,1,256]{3,1,2,0:T(8,128)(2,1)} %get-tuple-element.216) | copy-start | bytes 18874372 | tf_op jit(solution)/shard_map/while
  78.4 4.3 %copy-start.2 = (bf16[4,3072,1,256]{3,1,2,0:T(8,128)(2,1)S(1)}, bf16[4,3072,1,256]{3,1,2,0:T(8,128)(2,1)}, u32[]{:S(2)}) copy-start(bf16[4,3072,1,256]{3,1,2,0:T(8,128)(2,1)} %get-tuple-element.216) | copy-start | bytes 18874372 | tf_op jit(solution)/shard_map/while
  98.5 4.3 %copy-start.2 = (bf16[4,3072,1,256]{3,1,2,0:T(8,128)(2,1)S(1)}, bf16[4,3072,1,256]{3,1,2,0:T(8,128)(2,1)}, u32[]{:S(2)}) copy-start(bf16[4,3072,1,256]{3,1,2,0:T(8,128)(2,1)} %get-tuple-element.216) | copy-start | bytes 18874372 | tf_op jit(solution)/shard_map/while
  118.6 4.3 %copy-start.2 = (bf16[4,3072,1,256]{3,1,2,0:T(8,128)(2,1)S(1)}, bf16[4,3072,1,256]{3,1,2,0:T(8,128)(2,1)}, u32[]{:S(2)}) copy-start(bf16[4,3072,1,256]{3,1,2,0:T(8,128)(2,1)} %get-tuple-element.216) | copy-start | bytes 18874372 | tf_op jit(solution)/shard_map/while
  126.8 1.5 copy-start.7
  137.4 99.1 %copy-start.9 = (f32[5120]{0:T(1024)S(1)}, f32[5120]{0:T(1024)}, u32[]{:S(2)}) copy-start(f32[5120]{0:T(1024)} %param.20) | copy-start | bytes 61444
  234.1 2.0 copy-start.3
  236.5 3.1 copy-start.11
  239.6 69.2 %all-to-all-start = ((bf16[32,16,5120]{2,1,0:T(8,128)(2,1)}), bf16[32,16,5120]{2,1,0:T(8,128)(2,1)}, u32[]{:S(2)}, u32[]{:S(2)}) async-start(bf16[32,16,5120]{2,1,0:T(8,128)(2,1)} %stack.2), calls=%async_computation | async-start | bytes 10485760 | tf_op jit(solution)/shard_map/all_to_all | solution.py:173
  308.9 75.4 %copy-start.1 = (bf16[5120,256]{1,0:T(8,128)(2,1)S(1)}, bf16[5120,256]{1,0:T(8,128)(2,1)}, u32[]{:S(2)}) copy-start(bf16[5120,256]{1,0:T(8,128)(2,1)} %param.16) | copy-start | bytes 7864324
Sparse Core Ops, SparseCore 0:
  137.5 91.7 all-reduce.2
